TPU v7x, 128 devices: a whole 4x4x4 slice. The times are simulated.
128 devices in a mesh: sector: 8 (over z, core), mode: 16 (over y, x).
Axes of the slice: x: 4, y: 4, z: 4, core: 2. Of those that a mesh axis runs over, the one named last changes fastest.
Arguments:
- modes: bfloat16 [256, 3, 32, 80, 128], P('mode', None, 'sector'), may hold values from -0.1875 to 0.1875
- thickness: float32 [32, 80, 128], P('sector'), may hold values from -6 to 6
- stiff_taps: float32 [27], replicated, may hold values from -1.25 to 1.25
- mass_taps: float32 [27], replicated, may hold values from 0.02 to 0.2
- eigenvalues: float32 [256], P('mode'), may hold values from 0.5 to 2
Outputs:
- sensitivity: float32 [256, 256], P('sector', 'mode')
All inputs are finite; a program needn't handle non-finite values.
Results may differ from a plain program's by a relative error of at most 0.0029.
Values may be sent and summed in bfloat16 or wider, within the bound.
A program may use at most 64 MiB of HBM per device.

v0:
```python
import jax
import jax.numpy as jnp
from jax import lax
from jax.sharding import PartitionSpec as P


def extended(cells, sides, width):
    for axis, dim in sides:
        count = lax.axis_size(axis)
        ends = count - 1
        head = lax.slice_in_dim(cells, 0, width, axis=dim)
        tail = lax.slice_in_dim(cells, cells.shape[dim] - width, cells.shape[dim], axis=dim)
        cells = jnp.concatenate(
            [
                lax.ppermute(tail, axis, [(i, (i + 1) % count) for i in range(ends)]),
                cells,
                lax.ppermute(head, axis, [((i + 1) % count, i) for i in range(ends)]),
            ],
            axis=dim,
        )
    return cells


def stencil(field, padded_thick, stiff_taps, mass_taps, lams):
    size_x = field.shape[2] - 2
    size_y = field.shape[3] - 2
    size_z = field.shape[4] - 2
    shape_out = (field.shape[0], field.shape[1], size_x, size_y, size_z)
    centre = padded_thick[1 : 1 + size_x, 1 : 1 + size_y, 1 : 1 + size_z]
    stiff_acc = jnp.zeros(shape_out, jnp.float32)
    mass_acc = jnp.zeros(shape_out, jnp.float32)
    for aoff in range(3):
        for boff in range(3):
            for doff in range(3):
                index = 9 * aoff + 3 * boff + doff
                coeff = 0.5 * (
                    centre
                    + padded_thick[aoff : aoff + size_x, boff : boff + size_y, doff : doff + size_z]
                )
                moved = (
                    coeff
                    * field[:, :, aoff : aoff + size_x, boff : boff + size_y, doff : doff + size_z]
                )
                stiff_acc = stiff_acc + stiff_taps[index] * moved
                mass_acc = mass_acc + mass_taps[index] * moved
    return (stiff_acc - lams[:, None, None, None, None] * mass_acc).astype(jnp.bfloat16)


def spread(whole):
    sectors = lax.axis_size("sector")
    groups = lax.axis_size("mode")
    total = whole.shape[0]
    arranged = whole.reshape(sectors, total // sectors, groups, total // groups)
    arranged = arranged.transpose(0, 2, 1, 3).reshape(
        sectors * groups * (total // sectors), total // groups
    )
    return lax.psum_scatter(arranged, ("sector", "mode"), scatter_dimension=0, tiled=True)


def on_device(modes, thickness, stiff_taps, mass_taps, eigenvalues):
    local_modes = modes.shape[0]
    size_z = modes.shape[4]
    thick_rim = extended(thickness, (("sector", 0),), 1)
    padded_thick = jnp.pad(thick_rim, ((0, 0), (1, 1), (1, 1)))
    planes = extended(modes, (("sector", 2),), 1)
    field = jnp.pad(planes.astype(jnp.float32), ((0, 0), (0, 0), (0, 0), (1, 1), (1, 1)))
    loaded = stencil(field, padded_thick, stiff_taps, mass_taps, eigenvalues)
    flat_modes = modes.reshape(local_modes, -1, size_z)
    flat_loaded = loaded.reshape(local_modes, -1, size_z)
    all_modes, all_loaded = (
        lax.all_to_all(flat_modes, "mode", split_axis=1, concat_axis=0, tiled=True),
        lax.all_to_all(flat_loaded, "mode", split_axis=1, concat_axis=0, tiled=True),
    )
    whole = lax.dot_general(
        all_modes, all_loaded, (((1, 2), (1, 2)), ((), ())), preferred_element_type=jnp.float32
    )
    return spread(whole)


def solution(mesh):
    in_specs = (P("mode", None, "sector", None, None), P("sector", None, None), P(), P(), P("mode"))
    out_specs = P("sector", "mode")
    return jax.shard_map(
        on_device, mesh=mesh, in_specs=in_specs, out_specs=out_specs, check_vma=False
    )
```

profile of v0, /device:TPU:0, one launch (start us, length us, event | category | flops | bytes accessed | tf_op | source)
XLA Modules:
  0.0 861.1 jit_solution(12675278944696315850)
XLA Ops:
  6.5 0.8 fusion.56
  7.3 1.3 collective-permute-start
  8.6 1.3 collective-permute-start.1
  9.9 2.6 fusion.55
  12.6 5.3 collective-permute-start.2
  17.9 0.0 copy-start.3
  17.9 0.0 copy-start.4
  17.9 1.4 collective-permute-start.3
  19.4 6.5 copy.14
  25.9 7.1 all-to-all-start.1
  33.0 0.0 copy-start
  33.0 0.7 fusion.57
  33.7 0.7 fusion.58
  34.4 0.7 fusion.59
  35.2 0.7 fusion.60
  35.9 0.2 select_maximum_fusion
  36.1 0.2 fusion.53
  36.3 0.6 fusion.54
  37.0 0.9 maximum_convert_fusion
  38.0 96.1 %subtract_convert_fusion = bf16[16,3,4,80,128]{4,3,2,1,0:T(8,128)(2,1)S(1)} fusion(f32[16,3,6,80,128]{4,3,2,1,0:T(8,128)S(1)} %maximum_convert_fusion, f32[]{:T(128)} %bitcast.53, f32[]{:T(128)} %bitcast.52, f32[]{:T(128)} %bitcast.51, f32[]{:T(128)} %bitcast.50, f32[]{:T(128)} %bitcast.49, f32[]{:T(128)} %bitcast.48, f32[]{:T(128)} %bitcast.47, ...), kind=kLoop, calls=%fused_computation.51 | loop fusion | flops 267386880 | bytes 43746008 | tf_op jit(solution)/shard_map/convert_element_type | solution.py:46
  134.0 4.5 copy.12
  138.5 7.2 all-to-all-start
  145.7 0.0 reduce-scatter.4.cloned.1.call-start
  145.8 5.2 copy.15
  151.0 56.3 %all-to-all-done = bf16[16,960,128]{2,0,1:T(8,128)(2,1)} async-done(((bf16[16,960,128]{2,0,1:T(8,128)(2,1)}), bf16[16,960,128]{2,0,1:T(8,128)(2,1)}, u32[]{:S(2)}, u32[]{:S(2)}) %all-to-all-start) | async-done | bytes 3932192 | tf_op jit(solution)/shard_map/all_to_all | solution.py:72
  207.2 3.4 copy.13
  210.6 1.2 convolution_bitcast_fusion
  211.9 0.3 reshape.42
  212.1 2.0 copy.19
  214.1 0.0 reduce-scatter.4.cloned.1.call-update
  214.2 638.7 %reduce-scatter.4.cloned.1.call-done = f32[32,16]{1,0:T(8,128)} async-done(((f32[4096,16]{1,0:T(8,128)}), f32[32,16]{1,0:T(8,128)}) %reduce-scatter.4.cloned.1.call-update) | async-done | bytes 2064
  852.9 1.4 copy.18
  (14 shorter events, 0.0 us)
Async XLA Ops:
  7.3 28.5 %collective-permute-start = (f32[1,80,128]{2,1,0:T(8,128)S(1)}, f32[1,80,128]{2,1,0:T(8,128)S(1)}, u32[]{:S(2)}, u32[]{:S(2)}) collective-permute-start(f32[1,80,128]{2,1,0:T(8,128)S(1)} %get-tuple-element.34), channel_id=1, source_target_pairs={{0,16},{16,32},{32,48},{48,64},{64,80},{80,96},{96,112},{1,17},{17... | collective-permute-start | bytes 122888 | tf_op jit(solution)/shard_map/ppermute | solution.py:15
  8.6 27.2 %collective-permute-start.1 = (f32[1,80,128]{2,1,0:T(8,128)S(1)}, f32[1,80,128]{2,1,0:T(8,128)S(1)}, u32[]{:S(2)}, u32[]{:S(2)}) collective-permute-start(f32[1,80,128]{2,1,0:T(8,128)S(1)} %get-tuple-element.35), channel_id=1, source_target_pairs={{16,0},{32,16},{48,32},{64,48},{80,64},{96,80},{112,96},{17,1},{33... | collective-permute-start | bytes 122888 | tf_op jit(solution)/shard_map/ppermute | solution.py:17
  12.6 24.4 %collective-permute-start.2 = (bf16[16,3,1,80,128]{4,3,2,1,0:T(8,128)(2,1)}, bf16[16,3,1,80,128]{4,3,2,1,0:T(8,128)(2,1)S(1)}, u32[]{:S(2)}, u32[]{:S(2)}) collective-permute-start(bf16[16,3,1,80,128]{4,3,2,1,0:T(8,128)(2,1)} %get-tuple-element.5), channel_id=1, source_target_pairs={{0,16},{16,32},{32,48},{48,64},{64,80},{80,96},{96,112},{1,17},{17... | collective-permute-start | bytes 2949128 | tf_op jit(solution)/shard_map/ppermute | solution.py:15
  17.9 15.1 %copy-start.3 = (f32[27]{0:T(128)S(1)}, f32[27]{0:T(128)}, u32[]{:S(2)}) copy-start(f32[27]{0:T(128)} %param.7) | copy-start | bytes 328
  17.9 16.5 %copy-start.4 = (f32[27]{0:T(128)S(1)}, f32[27]{0:T(128)}, u32[]{:S(2)}) copy-start(f32[27]{0:T(128)} %param.8) | copy-start | bytes 328
  17.9 17.9 %copy-start.2 = (f32[4,80,128]{2,1,0:T(8,128)S(1)}, f32[4,80,128]{2,1,0:T(8,128)}, u32[]{:S(2)}) copy-start(f32[4,80,128]{2,1,0:T(8,128)} %param.6) | copy-start | bytes 491524
  17.9 19.1 %collective-permute-start.3 = (bf16[16,3,1,80,128]{4,3,2,1,0:T(8,128)(2,1)S(1)}, bf16[16,3,1,80,128]{4,3,2,1,0:T(8,128)(2,1)S(1)}, u32[]{:S(2)}, u32[]{:S(2)}) collective-permute-start(bf16[16,3,1,80,128]{4,3,2,1,0:T(8,128)(2,1)S(1)} %get-tuple-element.6), channel_id=1, source_target_pairs={{16,0},{32,16},{48,32},{64,48},{80,64},{96,80},{112,96},{17,1},{33... | collective-permute-start | bytes 2949128 | tf_op jit(solution)/shard_map/ppermute | solution.py:17
  25.9 112.6 %all-to-all-start.1 = ((bf16[16,960,128]{2,0,1:T(8,128)(2,1)}), bf16[16,960,128]{2,0,1:T(8,128)(2,1)}, u32[]{:S(2)}, u32[]{:S(2)}) async-start(bf16[16,960,128]{2,0,1:T(8,128)(2,1)} %bitcast.75), calls=%async_computation.1 | async-start | bytes 7864320 | tf_op jit(solution)/shard_map/all_to_all | solution.py:71
  33.0 4.0 copy-start
  37.0 1.0 copy-start.5
  138.5 68.7 %all-to-all-start = ((bf16[16,960,128]{2,0,1:T(8,128)(2,1)}), bf16[16,960,128]{2,0,1:T(8,128)(2,1)}, u32[]{:S(2)}, u32[]{:S(2)}) async-start(bf16[16,960,128]{2,0,1:T(8,128)(2,1)} %bitcast.76), calls=%async_computation | async-start | bytes 7864320 | tf_op jit(solution)/shard_map/all_to_all | solution.py:72
  145.7 707.1 %reduce-scatter.4.cloned.1.call-start = ((), (), s32[]{:S(2)}) async-start(), calls=%async_computation.3 | async-start | bytes 2113536
  207.2 3.4 copy-start.1
Sparse Core Ops, SparseCore 0:
  214.3 638.5 reduce-scatter.3
where the time goes:
time: 862 us; the launch traced here: 861 us
  waiting for transfers between devices  695 us (81%)
  other arithmetic  98.1 us (11%)
  local copies, waits for them, and re-layouts  29.5 us (3%)
  starting transfers between devices  23.6 us (3%)
  between operations  13.6 us (2%)
    unnamed x2, waiting for transfers between devices  639 us
    convert_element_type x1, other arithmetic, stencil(): (stiff_acc - lams[:, None, None, None, None] * mass_acc).astype(jnp.bfloa...  96.1 us
    all_to_all x1, waiting for transfers between devices, on_device(): lax.all_to_all(flat_loaded, 'mode', split_axis=1, concat_axis=0, tiled=True)  56.3 us
  transfers between devices with their start and end apart: 7, of which 2 were waited for; matrix products, arithmetic and copies ran while one was open for 14% of the time, Pallas kernels for 0%

commit v1 on v0

--- a/solution.py
+++ b/solution.py
@@ -2,6 +2,7 @@
 import jax.numpy as jnp
 from jax import lax
 from jax.sharding import PartitionSpec as P
+from jax.lax import all_to_all, axis_size
 
 
 def extended(cells, sides, width):
@@ -67,9 +68,15 @@
     loaded = stencil(field, padded_thick, stiff_taps, mass_taps, eigenvalues)
     flat_modes = modes.reshape(local_modes, -1, size_z)
     flat_loaded = loaded.reshape(local_modes, -1, size_z)
+    scan_the_point = lambda local_block, device_axis: jnp.concatenate(
+        all_to_all(
+            jnp.stack(jnp.split(local_block, axis_size(device_axis), axis=1)), device_axis, 0, 0
+        ),
+        axis=0,
+    )
     all_modes, all_loaded = (
         lax.all_to_all(flat_modes, "mode", split_axis=1, concat_axis=0, tiled=True),
-        lax.all_to_all(flat_loaded, "mode", split_axis=1, concat_axis=0, tiled=True),
+        scan_the_point(flat_loaded, "mode"),
     )
     whole = lax.dot_general(
         all_modes, all_loaded, (((1, 2), (1, 2)), ((), ())), preferred_element_type=jnp.float32

time: 862 us -> 872 us (1.012)
  local copies, waits for them, and re-layouts: 29.5 us -> 39.1 us
    unnamed x15 -> x30, local copies, waits for them, and re-layouts: 9.95 us -> 20.7 us
  transfers between devices with their start and end apart: 7 -> 7, of which waited for: 2 -> 2; matrix products, arithmetic and copies ran while one was open for 14% -> 15% of each run, Pallas kernels for 0% -> 0%
where the time goes in v1:
time: 872 us; the launch traced here: 871 us
  waiting for transfers between devices  695 us (80%)
  other arithmetic  98.1 us (11%)
  local copies, waits for them, and re-layouts  39.1 us (4%)
  starting transfers between devices  23.9 us (3%)
  between operations  13.6 us (2%)
    unnamed x2, waiting for transfers between devices  639 us
    convert_element_type x1, other arithmetic, stencil(): (stiff_acc - lams[:, None, None, None, None] * mass_acc).astype(jnp.bfloa...  96.1 us
    all_to_all x1, waiting for transfers between devices, on_device(): all_to_all(jnp.stack(jnp.split(local_block, axis_size(device_axis), axis=...  56 us
    unnamed x30, local copies, waits for them, and re-layouts  20.7 us
  transfers between devices with their start and end apart: 7, of which 2 were waited for; matrix products, arithmetic and copies ran while one was open for 15% of the time, Pallas kernels for 0%

profile of v1, /device:TPU:0, one launch (start us, length us, event | category | flops | bytes accessed | tf_op | source)
XLA Modules:
  0.0 870.6 jit_solution(18077665067913680038)
XLA Ops:
  6.5 0.8 fusion.72
  7.3 1.3 collective-permute-start
  8.6 1.3 collective-permute-start.1
  9.9 2.6 fusion.71
  12.6 5.3 collective-permute-start.2
  17.9 1.4 collective-permute-start.3
  19.4 6.5 copy.44
  25.9 7.1 all-to-all-start.1
  33.0 0.7 fusion.73
  34.4 0.7 fusion.75
  37.0 0.9 maximum_convert_fusion
  38.0 96.1 %subtract_convert_fusion = bf16[16,3,4,80,128]{4,3,2,1,0:T(8,128)(2,1)S(1)} fusion(f32[16,3,6,80,128]{4,3,2,1,0:T(8,128)S(1)} %maximum_convert_fusion, f32[]{:T(128)} %bitcast.53, f32[]{:T(128)} %bitcast.52, f32[]{:T(128)} %bitcast.51, f32[]{:T(128)} %bitcast.50, f32[]{:T(128)} %bitcast.49, f32[]{:T(128)} %bitcast.48, f32[]{:T(128)} %bitcast.47, ...), kind=kLoop, calls=%fused_computation.51 | loop fusion | flops 267386880 | bytes 43746008 | tf_op jit(solution)/shard_map/convert_element_type | solution.py:47
  134.0 2.5 copy.42
  138.0 0.7 fusion.40
  138.7 0.7 fusion.39
  139.4 0.7 fusion.38
  140.2 0.7 fusion.37
  142.3 0.7 fusion.34
  143.0 0.7 fusion.33
  143.7 0.7 fusion.32
  144.5 0.7 fusion.31
  145.9 0.7 fusion.29
  146.6 0.7 fusion.28
  147.3 0.7 fusion.27
  148.0 7.2 all-to-all-start
  155.5 5.2 copy.45
  160.7 56.0 %all-to-all-done = bf16[16,16,60,128]{3,1,2,0:T(8,128)(2,1)} async-done(((bf16[16,16,60,128]{3,1,2,0:T(8,128)(2,1)}), bf16[16,16,60,128]{3,1,2,0:T(8,128)(2,1)}, u32[]{:S(2)}, u32[]{:S(2)}) %all-to-all-start) | async-done | bytes 3932192 | tf_op jit(solution)/shard_map/all_to_all | solution.py:72
  216.7 3.4 copy.43
  220.2 1.2 convolution_bitcast_fusion
  221.7 2.0 copy.49
  223.7 638.7 %reduce-scatter.4.cloned.1.call-done = f32[32,16]{1,0:T(8,128)} async-done(((f32[4096,16]{1,0:T(8,128)}), f32[32,16]{1,0:T(8,128)}) %reduce-scatter.4.cloned.1.call-update) | async-done | bytes 2064
  862.4 1.4 copy.48
  (30 shorter events, 6.6 us)
Async XLA Ops:
  7.3 28.5 %collective-permute-start = (f32[1,80,128]{2,1,0:T(8,128)S(1)}, f32[1,80,128]{2,1,0:T(8,128)S(1)}, u32[]{:S(2)}, u32[]{:S(2)}) collective-permute-start(f32[1,80,128]{2,1,0:T(8,128)S(1)} %get-tuple-element.34), channel_id=1, source_target_pairs={{0,16},{16,32},{32,48},{48,64},{64,80},{80,96},{96,112},{1,17},{17... | collective-permute-start | bytes 122888 | tf_op jit(solution)/shard_map/ppermute | solution.py:16
  8.6 27.2 %collective-permute-start.1 = (f32[1,80,128]{2,1,0:T(8,128)S(1)}, f32[1,80,128]{2,1,0:T(8,128)S(1)}, u32[]{:S(2)}, u32[]{:S(2)}) collective-permute-start(f32[1,80,128]{2,1,0:T(8,128)S(1)} %get-tuple-element.35), channel_id=1, source_target_pairs={{16,0},{32,16},{48,32},{64,48},{80,64},{96,80},{112,96},{17,1},{33... | collective-permute-start | bytes 122888 | tf_op jit(solution)/shard_map/ppermute | solution.py:18
  12.6 24.4 %collective-permute-start.2 = (bf16[16,3,1,80,128]{4,3,2,1,0:T(8,128)(2,1)}, bf16[16,3,1,80,128]{4,3,2,1,0:T(8,128)(2,1)S(1)}, u32[]{:S(2)}, u32[]{:S(2)}) collective-permute-start(bf16[16,3,1,80,128]{4,3,2,1,0:T(8,128)(2,1)} %get-tuple-element.5), channel_id=1, source_target_pairs={{0,16},{16,32},{32,48},{48,64},{64,80},{80,96},{96,112},{1,17},{17... | collective-permute-start | bytes 2949128 | tf_op jit(solution)/shard_map/ppermute | solution.py:16
  17.9 15.1 %copy-start.3 = (f32[27]{0:T(128)S(1)}, f32[27]{0:T(128)}, u32[]{:S(2)}) copy-start(f32[27]{0:T(128)} %param.7) | copy-start | bytes 328
  17.9 16.5 %copy-start.4 = (f32[27]{0:T(128)S(1)}, f32[27]{0:T(128)}, u32[]{:S(2)}) copy-start(f32[27]{0:T(128)} %param.8) | copy-start | bytes 328
  17.9 17.9 %copy-start.2 = (f32[4,80,128]{2,1,0:T(8,128)S(1)}, f32[4,80,128]{2,1,0:T(8,128)}, u32[]{:S(2)}) copy-start(f32[4,80,128]{2,1,0:T(8,128)} %param.6) | copy-start | bytes 491524
  17.9 19.1 %collective-permute-start.3 = (bf16[16,3,1,80,128]{4,3,2,1,0:T(8,128)(2,1)S(1)}, bf16[16,3,1,80,128]{4,3,2,1,0:T(8,128)(2,1)S(1)}, u32[]{:S(2)}, u32[]{:S(2)}) collective-permute-start(bf16[16,3,1,80,128]{4,3,2,1,0:T(8,128)(2,1)S(1)} %get-tuple-element.6), channel_id=1, source_target_pairs={{16,0},{32,16},{48,32},{64,48},{80,64},{96,80},{112,96},{17,1},{33... | collective-permute-start | bytes 2949128 | tf_op jit(solution)/shard_map/ppermute | solution.py:18
  25.9 122.2 %all-to-all-start.1 = ((bf16[16,960,128]{2,0,1:T(8,128)(2,1)}), bf16[16,960,128]{2,0,1:T(8,128)(2,1)}, u32[]{:S(2)}, u32[]{:S(2)}) async-start(bf16[16,960,128]{2,0,1:T(8,128)(2,1)} %bitcast.136), calls=%async_computation.1 | async-start | bytes 7864320 | tf_op jit(solution)/shard_map/all_to_all | solution.py:78
  33.0 4.0 copy-start
  37.0 1.0 copy-start.5
  148.0 68.7 %all-to-all-start = ((bf16[16,16,60,128]{3,1,2,0:T(8,128)(2,1)}), bf16[16,16,60,128]{3,1,2,0:T(8,128)(2,1)}, u32[]{:S(2)}, u32[]{:S(2)}) async-start(bf16[16,16,60,128]{3,1,2,0:T(8,128)(2,1)} %fusion.27), calls=%async_computation | async-start | bytes 7864320 | tf_op jit(solution)/shard_map/all_to_all | solution.py:72
  155.3 707.2 %reduce-scatter.4.cloned.1.call-start = ((), (), s32[]{:S(2)}) async-start(), calls=%async_computation.3 | async-start | bytes 2113536
  216.7 3.4 copy-start.1
Sparse Core Ops, SparseCore 0:
  223.8 638.5 reduce-scatter.3
